TPU v7x, 512 devices: a whole 4x8x8 slice. The times are simulated.
512 devices in a mesh: gx: 32 (over x_lo, z, core), gy: 16 (over y, x_hi).
Axes of the slice: x: 4 (x_hi: 2, x_lo: 2; x = x_hi * 2 + x_lo), y: 8, z: 8, core: 2. Of those that a mesh axis runs over, the one named last changes fastest.
Arguments:
- currents: bfloat16 [1024, 512, 2, 128], P('gx', 'gy'), may hold values from -6 to 6
- box_count: int32 [1024, 512], P('gx', 'gy'), may hold values from 0 to 128, as said below
- aggregate: bfloat16 [256, 256], replicated, may hold values from -0.375 to 0.375
- near_blocks: bfloat16 [9, 256, 256], replicated, may hold values from -0.125 to 0.125
- low_translator: float32 [16, 2, 128], replicated, may hold values from -1.5 to 1.5
- child_to_parent: bfloat16 [4, 256, 512], replicated, may hold values from -0.1875 to 0.1875
- coarse_list: int32 [512, 256, 16], P('gx', 'gy'), may hold values from 0 to 4095
- coarse_kind: int32 [512, 256, 16], P('gx', 'gy'), may hold values from 0 to 63
- coarse_count: int32 [512, 256], P('gx', 'gy'), may hold values from 1 to 16, as said below
- up_translator: float32 [64, 2, 256], replicated, may hold values from -1.5 to 1.5
- parent_to_child: bfloat16 [4, 512, 256], replicated, may hold values from -0.25 to 0.25
- receive_map: bfloat16 [256, 256], replicated, may hold values from -0.375 to 0.375
Outputs:
- field: float32 [1024, 512, 2, 128], P('gx', 'gy')
Inputs may be any that keep to these rules, and one draw needn't show every extreme that they name: `box_count`: ground clutter makes some boxes full and most sparse; some box holds 128 unknowns and some none. `coarse_count`: some list uses all 16 entries.
All inputs are finite; a program needn't handle non-finite values.
Results may differ from a plain program's by a relative error of at most 0.0041.
Values may be sent and summed in bfloat16 or wider, within the bound.
A program may use at most 128 MiB of HBM per device.

v0:
```python
import jax
import jax.numpy as jnp
from jax import lax
from jax.sharding import PartitionSpec as P


def extended(cells, sides, width):
    for axis, dim in sides:
        count = lax.axis_size(axis)
        ends = count - 1
        head = lax.slice_in_dim(cells, 0, width, axis=dim)
        tail = lax.slice_in_dim(cells, cells.shape[dim] - width, cells.shape[dim], axis=dim)
        cells = jnp.concatenate(
            [
                lax.ppermute(tail, axis, [(i, (i + 1) % count) for i in range(ends)]),
                cells,
                lax.ppermute(head, axis, [((i + 1) % count, i) for i in range(ends)]),
            ],
            axis=dim,
        )
    return cells


def complex_flat(table, pattern, half):
    real_part = pattern[..., :half].astype(jnp.float32)
    imag_part = pattern[..., half:].astype(jnp.float32)
    first = table[..., :half] * real_part - table[..., half:] * imag_part
    second = table[..., :half] * imag_part + table[..., half:] * real_part
    return jnp.concatenate([first, second], axis=-1)


def make_patterns(block, aggregate):
    size_a, size_b = (block.shape[0], block.shape[1])
    flat_block = block.reshape(size_a * size_b, block.shape[2] * block.shape[3])
    result = jnp.dot(flat_block, aggregate, preferred_element_type=jnp.float32)
    return result.astype(jnp.bfloat16).reshape(size_a, size_b, aggregate.shape[1])


def translate_group(flat_group, lists, kinds, counts, table):
    rows_a, rows_b, slots = lists.shape
    kind_total, width_two = table.shape
    half = width_two // 2
    kind_ids = jnp.arange(kind_total, dtype=jnp.int32)[None, :]

    def accumulate(slot, total):
        index = lists[:, :, slot].reshape(rows_a * rows_b)
        source = jnp.take(flat_group, index, axis=0)
        choose = (kinds[:, :, slot].reshape(rows_a * rows_b)[:, None] == kind_ids).astype(
            jnp.float32
        )
        factors = jnp.dot(
            choose, table, precision=lax.Precision.HIGHEST, preferred_element_type=jnp.float32
        )
        term = complex_flat(factors, source, half)
        keep = (slot < counts).reshape(rows_a * rows_b)
        return total + jnp.where(keep[:, None], term, jnp.zeros_like(term))

    start = jnp.zeros((rows_a * rows_b, width_two), jnp.float32)
    result = lax.fori_loop(0, slots, accumulate, start)
    return result.astype(jnp.bfloat16).reshape(rows_a, rows_b, width_two)


def body(
    currents,
    box_count,
    aggregate,
    near_blocks,
    low_translator,
    child_to_parent,
    coarse_list,
    coarse_kind,
    coarse_count,
    up_translator,
    parent_to_child,
    receive_map,
):
    tile_x, tile_y = box_count.shape
    unknowns = currents.shape[-1]
    samples = low_translator.shape[-1]
    parent_samples = up_translator.shape[-1]
    kind_total = up_translator.shape[0]
    low_flat = low_translator.reshape(low_translator.shape[0], 2 * samples)
    mask = jnp.arange(unknowns, dtype=jnp.int32)[None, None, :] < box_count[:, :, None]
    live = jnp.where(mask[:, :, None, :], currents, jnp.zeros_like(currents))
    near_pad = extended(live, (("gx", 0), ("gy", 1)), 1)
    pattern = make_patterns(live, aggregate)
    pattern_pad = extended(pattern, (("gx", 0), ("gy", 1)), 2)
    lower_in = jnp.zeros((tile_x, tile_y, 2 * samples), jnp.float32)
    offset = 0
    for shift_x in range(-2, 3):
        for shift_y in range(-2, 3):
            if max(abs(shift_x), abs(shift_y)) < 2:
                continue
            source = pattern_pad[
                2 + shift_x : 2 + shift_x + tile_x, 2 + shift_y : 2 + shift_y + tile_y
            ]
            lower_in = lower_in + complex_flat(low_flat[offset], source, samples)
            offset += 1
    parents_x, parents_y = (tile_x // 2, tile_y // 2)
    children = pattern.reshape(parents_x, 2, parents_y, 2, 2 * samples)
    coarse_sum = jnp.zeros((parents_x * parents_y, 2 * parent_samples), jnp.float32)
    for half_x in range(2):
        for half_y in range(2):
            child = children[:, half_x, :, half_y].reshape(parents_x * parents_y, 2 * samples)
            coarse_sum = coarse_sum + jnp.dot(
                child, child_to_parent[2 * half_x + half_y], preferred_element_type=jnp.float32
            )
    coarse = coarse_sum.astype(jnp.bfloat16).reshape(parents_x, parents_y, 2 * parent_samples)
    group = lax.all_gather(coarse, "gy", axis=1, tiled=True)
    flat_group = group.reshape(group.shape[0] * group.shape[1], 2 * parent_samples)
    table = up_translator.reshape(kind_total, 2 * parent_samples)
    coarse_in = translate_group(flat_group, coarse_list, coarse_kind, coarse_count, table)
    coarse_flat = coarse_in.reshape(parents_x * parents_y, 2 * parent_samples)
    pieces = [
        jnp.dot(coarse_flat, parent_to_child[child_id], preferred_element_type=jnp.float32).reshape(
            parents_x, parents_y, 2 * samples
        )
        for child_id in range(4)
    ]
    rows_first = jnp.stack([pieces[0], pieces[1]], axis=2)
    rows_second = jnp.stack([pieces[2], pieces[3]], axis=2)
    from_parent = jnp.stack([rows_first, rows_second], axis=1).reshape(tile_x, tile_y, 2 * samples)
    incoming = (lower_in + from_parent).astype(jnp.bfloat16)
    field = jnp.dot(
        incoming.reshape(tile_x * tile_y, 2 * samples),
        receive_map,
        preferred_element_type=jnp.float32,
    )
    for shift_x in range(-1, 2):
        for shift_y in range(-1, 2):
            source = near_pad[
                1 + shift_x : 1 + shift_x + tile_x, 1 + shift_y : 1 + shift_y + tile_y
            ].reshape(tile_x * tile_y, 2 * unknowns)
            field = field + jnp.dot(
                source,
                near_blocks[3 * (shift_x + 1) + shift_y + 1],
                preferred_element_type=jnp.float32,
            )
    return field.reshape(tile_x, tile_y, 2, unknowns) * mask[:, :, None, :].astype(jnp.float32)


def solution(mesh):
    in_specs = (
        P("gx", "gy", None, None),
        P("gx", "gy"),
        P(),
        P(),
        P(),
        P(),
        P("gx", "gy", None),
        P("gx", "gy", None),
        P("gx", "gy"),
        P(),
        P(),
        P(),
    )
    out_specs = P("gx", "gy", None, None)
    return jax.shard_map(body, mesh=mesh, in_specs=in_specs, out_specs=out_specs, check_vma=False)
```

profile of v0, /device:TPU:8, one launch (start us, length us, event | category | flops | bytes accessed | tf_op | source)
XLA Modules:
  0.0 233.4 jit_solution(2320973562088822764)
XLA Ops:
  17.9 5.2 %collective-permute-start.4 = (bf16[1,32,2,128]{3,2,1,0:T(2,128)(2,1)S(1)}, bf16[1,32,2,128]{3,2,1,0:T(2,128)(2,1)S(1)}, u32[]{:S(2)}, u32[]{:S(2)}) collective-permute-start(bf16[1,32,2,128]{3,2,1,0:T(2,128)(2,1)S(1)} %get-tuple-element.260), channel_id=1, source_target_pairs={{0,16},{16,32},{32,48},{48,64},{64,80},{80,96},{96,112},{112,128},... | collective-permute-start | bytes 49160 | tf_op jit(solution)/shard_map/ppermute | solution.py:15
  24.8 2.7 %collective-permute-done.5 = bf16[1,32,2,128]{3,2,1,0:T(2,128)(2,1)S(1)} collective-permute-done((bf16[1,32,2,128]{3,2,1,0:T(2,128)(2,1)S(1)}, bf16[1,32,2,128]{3,2,1,0:T(2,128)(2,1)S(1)}, u32[]{:S(2)}, u32[]{:S(2)}) %collective-permute-start.5) | collective-permute-done | bytes 16416 | tf_op jit(solution)/shard_map/ppermute | solution.py:17
  27.5 4.9 %collective-permute-start.6 = (bf16[34,1,2,128]{3,2,1,0:T(2,128)(2,1)S(1)}, bf16[34,1,2,128]{3,2,1,0:T(2,128)(2,1)S(1)}, u32[]{:S(2)}, u32[]{:S(2)}) collective-permute-start(bf16[34,1,2,128]{3,2,1,0:T(2,128)(2,1)S(1)} %get-tuple-element.257), channel_id=1, source_target_pairs={{0,1},{1,2},{2,3},{3,4},{4,5},{5,6},{6,7},{7,8},{8,9},{9,10},{10,1... | collective-permute-start | bytes 52232 | tf_op jit(solution)/shard_map/ppermute | solution.py:15
  32.4 3.3 %collective-permute-start.7 = (bf16[34,1,2,128]{3,2,1,0:T(2,128)(2,1)S(1)}, bf16[34,1,2,128]{3,2,1,0:T(2,128)(2,1)S(1)}, u32[]{:S(2)}, u32[]{:S(2)}) collective-permute-start(bf16[34,1,2,128]{3,2,1,0:T(2,128)(2,1)S(1)} %get-tuple-element.256), channel_id=1, source_target_pairs={{1,0},{2,1},{3,2},{4,3},{5,4},{6,5},{7,6},{8,7},{9,8},{10,9},{11,1... | collective-permute-start | bytes 52232 | tf_op jit(solution)/shard_map/ppermute | solution.py:17
  35.8 2.4 %pad_maximum_fusion.3 = (bf16[32,32,2,128]{3,2,1,0:T(2,128)(2,1)}, bf16[32,32,2,128]{3,2,1,0:T(2,128)(2,1)}) fusion(bf16[1,32,2,128]{3,2,1,0:T(2,128)(2,1)S(1)} %collective-permute-done.5, bf16[32,32,2,128]{3,2,1,0:T(2,128)(2,1)S(1)} %broadcast_select_fusion.1, bf16[1,32,2,128]{3,2,1,0:T(2,128)(2,1)S(1)} %collective-permute-done.4), kind=kLoop, calls=%fused_computation.176 | loop fusion | flops 524288 | bytes 1605632 | tf_op jit(solution)/shard_map/concatenate | solution.py:13
  38.2 4.0 %collective-permute-start.2 = (bf16[36,2,256]{2,1,0:T(2,128)(2,1)S(1)}, bf16[36,2,256]{2,1,0:T(2,128)(2,1)S(1)}, u32[]{:S(2)}, u32[]{:S(2)}) collective-permute-start(bf16[36,2,256]{2,1,0:T(2,128)(2,1)S(1)} %get-tuple-element.242), channel_id=1, source_target_pairs={{0,1},{1,2},{2,3},{3,4},{4,5},{5,6},{6,7},{7,8},{8,9},{9,10},{10,1... | collective-permute-start | bytes 110600 | tf_op jit(solution)/shard_map/ppermute | solution.py:15
  42.3 4.4 %collective-permute-start.3 = (bf16[36,2,256]{2,1,0:T(2,128)(2,1)S(1)}, bf16[36,2,256]{2,1,0:T(2,128)(2,1)S(1)}, u32[]{:S(2)}, u32[]{:S(2)}) collective-permute-start(bf16[36,2,256]{2,1,0:T(2,128)(2,1)S(1)} %get-tuple-element.243), channel_id=1, source_target_pairs={{1,0},{2,1},{3,2},{4,3},{5,4},{6,5},{7,6},{8,7},{9,8},{10,9},{11,1... | collective-permute-start | bytes 110600 | tf_op jit(solution)/shard_map/ppermute | solution.py:17
  48.9 2.1 pad_maximum_fusion.2
  51.1 4.4 %fusion.115 = (bf16[32,32,2,128]{3,2,1,0:T(2,128)(2,1)}, bf16[32,32,2,128]{3,2,1,0:T(2,128)(2,1)}, bf16[32,32,2,128]{3,2,1,0:T(2,128)(2,1)}, bf16[32,32,2,128]{3...) fusion(bf16[34,33,2,128]{3,2,1,0:T(2,128)(2,1)S(1)} %get-tuple-element.254, ...), kind=kLoop, calls=%fused_computation.264 | loop fusion | bytes 6291456 | tf_op jit(solution)/shard_map/slice | solution.py:131
  57.7 2.1 fusion.24
  59.8 2.1 fusion.26
  62.0 2.5 %fusion.32 = (f32[32,32,128]{2,1,0:T(8,128)}, f32[32,32,128]{2,1,0:T(8,128)}, f32[32,32,128]{2,1,0:T(8,128)}, f32[32,32,128]{2,1,0:T(8,128)}, f32[32,32,128]{2,1,0:T(8,128)}, /*index=5*/f32[32,32,128]{2,1,0:T(8,128)}) fusion(f32[128]{0:T(128)S(1)} %get-tuple-element.292, f32[128]{0:T(128)S(1)} %get-tuple-element.293, ...), kind=kLoop, calls=%fused_computation.134 | loop fusion | flops 3145728 | bytes 4721664 | tf_op jit(solution)/shard_map/sub | solution.py:27
  64.4 2.4 %fusion.30 = (f32[32,32,128]{2,1,0:T(8,128)}, f32[32,32,128]{2,1,0:T(8,128)}, f32[32,32,128]{2,1,0:T(8,128)}, f32[32,32,128]{2,1,0:T(8,128)}, f32[32,32,128]{2,1,0:T(8,128)}, /*index=5*/f32[32,32,128]{2,1,0:T(8,128)}) fusion(f32[128]{0:T(128)S(1)} %get-tuple-element.294, f32[128]{0:T(128)S(1)} %get-tuple-element.295, ...), kind=kLoop, calls=%fused_computation.132 | loop fusion | flops 3145728 | bytes 4721664 | tf_op jit(solution)/shard_map/sub | solution.py:27
  66.8 58.1 %all-gather.2.cloned.1.call-done = bf16[16,256,512]{2,1,0:T(8,128)(2,1)} async-done(((bf16[16,16,512]{2,1,0:T(8,128)(2,1)}), bf16[16,256,512]{2,1,0:T(8,128)(2,1)}) %all-gather.2.cloned.1.call-update) | async-done | bytes 4194320 | tf_op jit(solution)/shard_map/all_gather | solution.py:109
  125.0 81.5 %while.14 = (s32[]{:T(128)}, f32[256,512]{1,0:T(8,128)S(1)}, s32[16,16]{1,0:T(8,128)S(1)}, s32[16,16,16]{1,0,2:T(8,128)S(1)}, f32[64,512]{1,0:T(8,128)S(1)}, /*i...) while((s32[]{:T(128)}, f32[256,512]{1,0:T(8,128)S(1)}, ...), condition=%wide.region_1.2_spmd.clone, body=%wide.region_0.1_spmd.clone.sunk | while | flops 101862912 | bytes 4610671 | solution.py:59
  125.1 4.0 %gather_fusion = bf16[256,512]{1,0:T(8,128)(2,1)S(1)} fusion(bf16[4096,512]{1,0:T(8,128)(2,1)} %get-tuple-element.384, s32[1024]{0:T(1024)S(1)} %pad_clamp_fusion.2), kind=kCustom, calls=%fused_computation.clone.clone.1 | custom fusion | bytes 525312 | tf_op jit(solution)/shard_map/while/body/eval_jaxpr/jit(_take)/gather | solution.py:47
  130.2 3.9 %gather_fusion = bf16[256,512]{1,0:T(8,128)(2,1)S(1)} fusion(bf16[4096,512]{1,0:T(8,128)(2,1)} %get-tuple-element.384, s32[1024]{0:T(1024)S(1)} %pad_clamp_fusion.2), kind=kCustom, calls=%fused_computation.clone.clone.1 | custom fusion | bytes 525312 | tf_op jit(solution)/shard_map/while/body/eval_jaxpr/jit(_take)/gather | solution.py:47
  135.3 3.9 %gather_fusion = bf16[256,512]{1,0:T(8,128)(2,1)S(1)} fusion(bf16[4096,512]{1,0:T(8,128)(2,1)} %get-tuple-element.384, s32[1024]{0:T(1024)S(1)} %pad_clamp_fusion.2), kind=kCustom, calls=%fused_computation.clone.clone.1 | custom fusion | bytes 525312 | tf_op jit(solution)/shard_map/while/body/eval_jaxpr/jit(_take)/gather | solution.py:47
  140.4 3.9 %gather_fusion = bf16[256,512]{1,0:T(8,128)(2,1)S(1)} fusion(bf16[4096,512]{1,0:T(8,128)(2,1)} %get-tuple-element.384, s32[1024]{0:T(1024)S(1)} %pad_clamp_fusion.2), kind=kCustom, calls=%fused_computation.clone.clone.1 | custom fusion | bytes 525312 | tf_op jit(solution)/shard_map/while/body/eval_jaxpr/jit(_take)/gather | solution.py:47
  145.5 3.9 %gather_fusion = bf16[256,512]{1,0:T(8,128)(2,1)S(1)} fusion(bf16[4096,512]{1,0:T(8,128)(2,1)} %get-tuple-element.384, s32[1024]{0:T(1024)S(1)} %pad_clamp_fusion.2), kind=kCustom, calls=%fused_computation.clone.clone.1 | custom fusion | bytes 525312 | tf_op jit(solution)/shard_map/while/body/eval_jaxpr/jit(_take)/gather | solution.py:47
  150.6 3.9 %gather_fusion = bf16[256,512]{1,0:T(8,128)(2,1)S(1)} fusion(bf16[4096,512]{1,0:T(8,128)(2,1)} %get-tuple-element.384, s32[1024]{0:T(1024)S(1)} %pad_clamp_fusion.2), kind=kCustom, calls=%fused_computation.clone.clone.1 | custom fusion | bytes 525312 | tf_op jit(solution)/shard_map/while/body/eval_jaxpr/jit(_take)/gather | solution.py:47
  155.7 3.9 %gather_fusion = bf16[256,512]{1,0:T(8,128)(2,1)S(1)} fusion(bf16[4096,512]{1,0:T(8,128)(2,1)} %get-tuple-element.384, s32[1024]{0:T(1024)S(1)} %pad_clamp_fusion.2), kind=kCustom, calls=%fused_computation.clone.clone.1 | custom fusion | bytes 525312 | tf_op jit(solution)/shard_map/while/body/eval_jaxpr/jit(_take)/gather | solution.py:47
  160.8 3.9 %gather_fusion = bf16[256,512]{1,0:T(8,128)(2,1)S(1)} fusion(bf16[4096,512]{1,0:T(8,128)(2,1)} %get-tuple-element.384, s32[1024]{0:T(1024)S(1)} %pad_clamp_fusion.2), kind=kCustom, calls=%fused_computation.clone.clone.1 | custom fusion | bytes 525312 | tf_op jit(solution)/shard_map/while/body/eval_jaxpr/jit(_take)/gather | solution.py:47
  165.9 3.9 %gather_fusion = bf16[256,512]{1,0:T(8,128)(2,1)S(1)} fusion(bf16[4096,512]{1,0:T(8,128)(2,1)} %get-tuple-element.384, s32[1024]{0:T(1024)S(1)} %pad_clamp_fusion.2), kind=kCustom, calls=%fused_computation.clone.clone.1 | custom fusion | bytes 525312 | tf_op jit(solution)/shard_map/while/body/eval_jaxpr/jit(_take)/gather | solution.py:47
  171.0 3.9 %gather_fusion = bf16[256,512]{1,0:T(8,128)(2,1)S(1)} fusion(bf16[4096,512]{1,0:T(8,128)(2,1)} %get-tuple-element.384, s32[1024]{0:T(1024)S(1)} %pad_clamp_fusion.2), kind=kCustom, calls=%fused_computation.clone.clone.1 | custom fusion | bytes 525312 | tf_op jit(solution)/shard_map/while/body/eval_jaxpr/jit(_take)/gather | solution.py:47
  176.1 3.9 %gather_fusion = bf16[256,512]{1,0:T(8,128)(2,1)S(1)} fusion(bf16[4096,512]{1,0:T(8,128)(2,1)} %get-tuple-element.384, s32[1024]{0:T(1024)S(1)} %pad_clamp_fusion.2), kind=kCustom, calls=%fused_computation.clone.clone.1 | custom fusion | bytes 525312 | tf_op jit(solution)/shard_map/while/body/eval_jaxpr/jit(_take)/gather | solution.py:47
  181.1 3.9 %gather_fusion = bf16[256,512]{1,0:T(8,128)(2,1)S(1)} fusion(bf16[4096,512]{1,0:T(8,128)(2,1)} %get-tuple-element.384, s32[1024]{0:T(1024)S(1)} %pad_clamp_fusion.2), kind=kCustom, calls=%fused_computation.clone.clone.1 | custom fusion | bytes 525312 | tf_op jit(solution)/shard_map/while/body/eval_jaxpr/jit(_take)/gather | solution.py:47
  186.2 3.9 %gather_fusion = bf16[256,512]{1,0:T(8,128)(2,1)S(1)} fusion(bf16[4096,512]{1,0:T(8,128)(2,1)} %get-tuple-element.384, s32[1024]{0:T(1024)S(1)} %pad_clamp_fusion.2), kind=kCustom, calls=%fused_computation.clone.clone.1 | custom fusion | bytes 525312 | tf_op jit(solution)/shard_map/while/body/eval_jaxpr/jit(_take)/gather | solution.py:47
  191.3 3.9 %gather_fusion = bf16[256,512]{1,0:T(8,128)(2,1)S(1)} fusion(bf16[4096,512]{1,0:T(8,128)(2,1)} %get-tuple-element.384, s32[1024]{0:T(1024)S(1)} %pad_clamp_fusion.2), kind=kCustom, calls=%fused_computation.clone.clone.1 | custom fusion | bytes 525312 | tf_op jit(solution)/shard_map/while/body/eval_jaxpr/jit(_take)/gather | solution.py:47
  196.4 3.9 %gather_fusion = bf16[256,512]{1,0:T(8,128)(2,1)S(1)} fusion(bf16[4096,512]{1,0:T(8,128)(2,1)} %get-tuple-element.384, s32[1024]{0:T(1024)S(1)} %pad_clamp_fusion.2), kind=kCustom, calls=%fused_computation.clone.clone.1 | custom fusion | bytes 525312 | tf_op jit(solution)/shard_map/while/body/eval_jaxpr/jit(_take)/gather | solution.py:47
  201.5 3.9 %gather_fusion = bf16[256,512]{1,0:T(8,128)(2,1)S(1)} fusion(bf16[4096,512]{1,0:T(8,128)(2,1)} %get-tuple-element.384, s32[1024]{0:T(1024)S(1)} %pad_clamp_fusion.2), kind=kCustom, calls=%fused_computation.clone.clone.1 | custom fusion | bytes 525312 | tf_op jit(solution)/shard_map/while/body/eval_jaxpr/jit(_take)/gather | solution.py:47
  209.5 6.5 %fusion.74 = f32[1024,256]{1,0:T(8,128)S(1)} fusion(bf16[256,256]{1,0:T(8,128)(2,1)S(1)} %copy-done.15, f32[1024,256]{1,0:T(8,128)S(1)} %reshape.262, f32[1024,128]{1,0:T(8,128)} %bitcast.276, f32[1024,128]{1,0:T(8,128)} %bitcast.277, f32[1024,128]{1,0:T(8,128)} %bitcast.278, f32[1024,128]{1,0:T(8,128)} %bitcast.279, f32[1024,128]{1,0:T(8,128)} %bitcast.289, ...), kind=kOutput, calls=%fused_computation.182 | convolution fusion | flops 142868480 | bytes 19005440 | tf_op jit(solution)/shard_map/dot_general | solution.py:124
  (307 shorter events, 48.2 us)
Async XLA Ops:
  6.5 3.7 %copy-start = (bf16[256,256]{1,0:T(8,128)(2,1)S(1)}, bf16[256,256]{1,0:T(8,128)(2,1)}, u32[]{:S(2)}) copy-start(bf16[256,256]{1,0:T(8,128)(2,1)} %param.16) | copy-start | bytes 393220
  6.5 118.4 %all-gather.2.cloned.1.call-start = ((), (), s32[]{:S(2)}) async-start(), calls=%async_computation | async-start | bytes 4456448 | tf_op jit(solution)/shard_map/all_gather | solution.py:109
  11.9 1.2 copy-start.13
  13.8 10.6 %copy-start.19 = (f32[16,2,128]{2,1,0:T(2,128)S(1)}, f32[16,2,128]{2,1,0:T(2,128)}, u32[]{:S(2)}) copy-start(f32[16,2,128]{2,1,0:T(2,128)} %param.18) | copy-start | bytes 49156
  13.8 10.7 %copy-start.16 = (f32[64,2,256]{2,1,0:T(2,128)S(1)}, f32[64,2,256]{2,1,0:T(2,128)}, u32[]{:S(2)}) copy-start(f32[64,2,256]{2,1,0:T(2,128)} %param.23) | copy-start | bytes 393220
  13.8 10.7 %copy-start.17 = (s32[16,16,16]{2,1,0:T(8,128)S(1)}, s32[16,16,16]{2,1,0:T(8,128)}, u32[]{:S(2)}) copy-start(s32[16,16,16]{2,1,0:T(8,128)} %param.21) | copy-start | bytes 49156
  13.8 10.8 %copy-start.18 = (s32[16,16,16]{2,1,0:T(8,128)S(1)}, s32[16,16,16]{2,1,0:T(8,128)}, u32[]{:S(2)}) copy-start(s32[16,16,16]{2,1,0:T(8,128)} %param.20) | copy-start | bytes 49156
  14.8 23.3 %collective-permute-start = (bf16[2,32,256]{2,1,0:T(8,128)(2,1)S(1)}, bf16[2,32,256]{2,1,0:T(8,128)(2,1)S(1)}, u32[]{:S(2)}, u32[]{:S(2)}) collective-permute-start(bf16[2,32,256]{2,1,0:T(8,128)(2,1)S(1)} %bitcast.304), channel_id=1, source_target_pairs={{0,16},{16,32},{32,48},{48,64},{64,80},{80,96},{96,112},{112,128},... | collective-permute-start | bytes 98312 | tf_op jit(solution)/shard_map/ppermute | solution.py:15
  16.6 21.6 %collective-permute-start.1 = (bf16[2,32,256]{2,1,0:T(8,128)(2,1)S(1)}, bf16[2,32,256]{2,1,0:T(8,128)(2,1)S(1)}, u32[]{:S(2)}, u32[]{:S(2)}) collective-permute-start(bf16[2,32,256]{2,1,0:T(8,128)(2,1)S(1)} %bitcast.303), channel_id=1, source_target_pairs={{16,0},{32,16},{48,32},{64,48},{80,64},{96,80},{112,96},{128,112},... | collective-permute-start | bytes 98312 | tf_op jit(solution)/shard_map/ppermute | solution.py:17
  17.9 6.8 %collective-permute-start.4 = (bf16[1,32,2,128]{3,2,1,0:T(2,128)(2,1)S(1)}, bf16[1,32,2,128]{3,2,1,0:T(2,128)(2,1)S(1)}, u32[]{:S(2)}, u32[]{:S(2)}) collective-permute-start(bf16[1,32,2,128]{3,2,1,0:T(2,128)(2,1)S(1)} %get-tuple-element.260), channel_id=1, source_target_pairs={{0,16},{16,32},{32,48},{48,64},{64,80},{80,96},{96,112},{112,128},... | collective-permute-start | bytes 49160 | tf_op jit(solution)/shard_map/ppermute | solution.py:15
  23.1 4.3 %collective-permute-start.5 = (bf16[1,32,2,128]{3,2,1,0:T(2,128)(2,1)S(1)}, bf16[1,32,2,128]{3,2,1,0:T(2,128)(2,1)S(1)}, u32[]{:S(2)}, u32[]{:S(2)}) collective-permute-start(bf16[1,32,2,128]{3,2,1,0:T(2,128)(2,1)S(1)} %get-tuple-element.261), channel_id=1, source_target_pairs={{16,0},{32,16},{48,32},{64,48},{80,64},{96,80},{112,96},{128,112},... | collective-permute-start | bytes 49160 | tf_op jit(solution)/shard_map/ppermute | solution.py:17
  27.5 21.5 %collective-permute-start.6 = (bf16[34,1,2,128]{3,2,1,0:T(2,128)(2,1)S(1)}, bf16[34,1,2,128]{3,2,1,0:T(2,128)(2,1)S(1)}, u32[]{:S(2)}, u32[]{:S(2)}) collective-permute-start(bf16[34,1,2,128]{3,2,1,0:T(2,128)(2,1)S(1)} %get-tuple-element.257), channel_id=1, source_target_pairs={{0,1},{1,2},{2,3},{3,4},{4,5},{5,6},{6,7},{7,8},{8,9},{9,10},{10,1... | collective-permute-start | bytes 52232 | tf_op jit(solution)/shard_map/ppermute | solution.py:15
  32.4 16.5 %collective-permute-start.7 = (bf16[34,1,2,128]{3,2,1,0:T(2,128)(2,1)S(1)}, bf16[34,1,2,128]{3,2,1,0:T(2,128)(2,1)S(1)}, u32[]{:S(2)}, u32[]{:S(2)}) collective-permute-start(bf16[34,1,2,128]{3,2,1,0:T(2,128)(2,1)S(1)} %get-tuple-element.256), channel_id=1, source_target_pairs={{1,0},{2,1},{3,2},{4,3},{5,4},{6,5},{7,6},{8,7},{9,8},{10,9},{11,1... | collective-permute-start | bytes 52232 | tf_op jit(solution)/shard_map/ppermute | solution.py:17
  38.2 17.3 %collective-permute-start.2 = (bf16[36,2,256]{2,1,0:T(2,128)(2,1)S(1)}, bf16[36,2,256]{2,1,0:T(2,128)(2,1)S(1)}, u32[]{:S(2)}, u32[]{:S(2)}) collective-permute-start(bf16[36,2,256]{2,1,0:T(2,128)(2,1)S(1)} %get-tuple-element.242), channel_id=1, source_target_pairs={{0,1},{1,2},{2,3},{3,4},{4,5},{5,6},{6,7},{7,8},{8,9},{9,10},{10,1... | collective-permute-start | bytes 110600 | tf_op jit(solution)/shard_map/ppermute | solution.py:15
  42.3 13.2 %collective-permute-start.3 = (bf16[36,2,256]{2,1,0:T(2,128)(2,1)S(1)}, bf16[36,2,256]{2,1,0:T(2,128)(2,1)S(1)}, u32[]{:S(2)}, u32[]{:S(2)}) collective-permute-start(bf16[36,2,256]{2,1,0:T(2,128)(2,1)S(1)} %get-tuple-element.243), channel_id=1, source_target_pairs={{1,0},{2,1},{3,2},{4,3},{5,4},{6,5},{7,6},{8,7},{9,8},{10,9},{11,1... | collective-permute-start | bytes 110600 | tf_op jit(solution)/shard_map/ppermute | solution.py:17
  64.4 60.5 %copy-start.14 = (s32[16,16]{1,0:T(8,128)S(1)}, s32[16,16]{1,0:T(8,128)}, u32[]{:S(2)}) copy-start(s32[16,16]{1,0:T(8,128)} %param.22) | copy-start | bytes 3076
  125.0 81.6 %copy-start.12 = (bf16[4,512,256]{2,1,0:T(8,128)(2,1)S(1)}, bf16[4,512,256]{2,1,0:T(8,128)(2,1)}, u32[]{:S(2)}) copy-start(bf16[4,512,256]{2,1,0:T(8,128)(2,1)} %param.24) | copy-start | bytes 3145732
  208.5 1.0 copy-start.1
  208.5 1.1 copy-start.15
  209.5 6.5 %copy-start.10 = (bf16[32,32,2,128]{3,2,1,0:T(2,128)(2,1)S(1)}, bf16[32,32,2,128]{3,2,1,0:T(2,128)(2,1)}, u32[]{:S(2)}) copy-start(bf16[32,32,2,128]{3,2,1,0:T(2,128)(2,1)} %get-tuple-element.302) | copy-start | bytes 1572868
  209.5 6.5 %copy-start.11 = (bf16[9,256,256]{2,1,0:T(8,128)(2,1)S(1)}, bf16[9,256,256]{2,1,0:T(8,128)(2,1)}, u32[]{:S(2)}) copy-start(bf16[9,256,256]{2,1,0:T(8,128)(2,1)} %param.17) | copy-start | bytes 3538948
  216.1 1.0 copy-start.4
  217.1 1.0 copy-start.9
  218.2 1.0 copy-start.8
  219.5 1.0 copy-start.7
  220.6 1.0 copy-start.6
  221.6 1.0 copy-start.3
  222.7 1.0 copy-start.5
  224.0 1.0 copy-start.2
Sparse Core Ops, SparseCore 0:
  14.9 109.9 all-gather.1
where the time goes:
time: 235 us; the launch traced here: 233 us
  local copies, waits for them, and re-layouts  83.8 us (36%)
  waiting for transfers between devices  60.8 us (26%)
  other arithmetic  29.2 us (12%)
  starting transfers between devices  26.2 us (11%)
  matrix products  18.6 us (8%)
  between operations  13.9 us (6%)
    gather x16, local copies, waits for them, and re-layouts, accumulate(): source = jnp.take(flat_group, index, axis=0)  63.1 us
    all_gather x1, waiting for transfers between devices, body(): group = lax.all_gather(coarse, 'gy', axis=1, tiled=True)  58.1 us
    ppermute x4, starting transfers between devices, extended(): lax.ppermute(tail, axis, [(i, (i + 1) % count) for i in range(ends)])  15.9 us
    sub x23, other arithmetic, complex_flat(): first = table[..., :half] * real_part - table[..., half:] * imag_part  14.4 us
    ppermute x4, starting transfers between devices, extended(): lax.ppermute(head, axis, [((i + 1) % count, i) for i in range(ends)])  10.3 us
    unnamed x47, local copies, waits for them, and re-layouts  7.43 us
    dot_general x16, matrix products, accumulate(): jnp.dot(choose, table, precision=lax.Precision.HIGHEST, preferred_element...  6.53 us
    dot_general x1, matrix products, body(): jnp.dot(incoming.reshape(tile_x * tile_y, 2 * samples), receive_map, pref...  6.53 us
  transfers between devices with their start and end apart: 9, of which 2 were waited for; matrix products, arithmetic and copies ran while one was open for 10% of the time, Pallas kernels for 0%

commit v1 on v0

--- a/solution.py
+++ b/solution.py
@@ -106,7 +106,9 @@
                 child, child_to_parent[2 * half_x + half_y], preferred_element_type=jnp.float32
             )
     coarse = coarse_sum.astype(jnp.bfloat16).reshape(parents_x, parents_y, 2 * parent_samples)
-    group = lax.all_gather(coarse, "gy", axis=1, tiled=True)
+    group = jnp.concatenate(
+        lax.all_to_all(jnp.stack([coarse] * lax.axis_size("gy")), "gy", 0, 0), axis=1
+    )
     flat_group = group.reshape(group.shape[0] * group.shape[1], 2 * parent_samples)
     table = up_translator.reshape(kind_total, 2 * parent_samples)
     coarse_in = translate_group(flat_group, coarse_list, coarse_kind, coarse_count, table)

time: 235 us -> 254 us (1.081)
  the two profiles are of different devices: /device:TPU:8 before, /device:TPU:454 now
where the time goes in v1:
time: 254 us; the launch traced here: 252 us
  local copies, waits for them, and re-layouts  104 us (41%)
  waiting for transfers between devices  64.5 us (25%)
  starting transfers between devices  36 us (14%)
  other arithmetic  28.9 us (11%)
  matrix products  17.8 us (7%)
    gather x16, local copies, waits for them, and re-layouts, accumulate(): source = jnp.take(flat_group, index, axis=0)  63 us
    ppermute x4, waiting for transfers between devices, extended(): lax.ppermute(tail, axis, [(i, (i + 1) % count) for i in range(ends)])  61 us
    ppermute x4, starting transfers between devices, extended(): lax.ppermute(head, axis, [((i + 1) % count, i) for i in range(ends)])  14.3 us
    sub x23, other arithmetic, complex_flat(): first = table[..., :half] * real_part - table[..., half:] * imag_part  14.3 us
    dynamic_slice x16, local copies, waits for them, and re-layouts, accumulate(): index = lists[:, :, slot].reshape(rows_a * rows_b)  11.6 us
    ppermute x4, starting transfers between devices, extended(): lax.ppermute(tail, axis, [(i, (i + 1) % count) for i in range(ends)])  11.5 us
    all_to_all x1, starting transfers between devices, body(): lax.all_to_all(jnp.stack([coarse] * lax.axis_size('gy')), 'gy', 0, 0)  10.2 us
    unnamed x47, local copies, waits for them, and re-layouts  8.57 us
  transfers between devices with their start and end apart: 9, of which 2 were waited for; matrix products, arithmetic and copies ran while one was open for 9% of the time, Pallas kernels for 0%

profile of v1, /device:TPU:454, one launch (start us, length us, event | category | flops | bytes accessed | tf_op | source)
XLA Modules:
  0.0 252.3 jit_solution(17028456604925404840)
XLA Ops:
  7.5 2.6 %stack.18 = bf16[16,16,16,512]{3,2,1,0:T(8,128)(2,1)} broadcast(bf16[16,16,512]{2,1,0:T(8,128)(2,1)S(1)} %bitcast.298), dimensions={1,2,3} | broadcast | bytes 4456448 | tf_op jit(solution)/shard_map/stack | solution.py:110
  10.0 10.2 %all-to-all-start = ((bf16[16,16,16,512]{3,2,1,0:T(8,128)(2,1)}), bf16[16,16,16,512]{3,2,1,0:T(8,128)(2,1)}, u32[]{:S(2)}, u32[]{:S(2)}) async-start(bf16[16,16,16,512]{3,2,1,0:T(8,128)(2,1)} %stack.18), calls=%async_computation | async-start | bytes 8388608 | tf_op jit(solution)/shard_map/all_to_all | solution.py:110
  22.2 3.6 %collective-permute-start.1 = (bf16[2,32,256]{2,1,0:T(8,128)(2,1)S(1)}, bf16[2,32,256]{2,1,0:T(8,128)(2,1)S(1)}, u32[]{:S(2)}, u32[]{:S(2)}) collective-permute-start(bf16[2,32,256]{2,1,0:T(8,128)(2,1)S(1)} %bitcast.305), channel_id=1, source_target_pairs={{16,0},{32,16},{48,32},{64,48},{80,64},{96,80},{112,96},{128,112},... | collective-permute-start | bytes 98312 | tf_op jit(solution)/shard_map/ppermute | solution.py:17
  27.8 3.6 %collective-permute-start.5 = (bf16[1,32,2,128]{3,2,1,0:T(2,128)(2,1)S(1)}, bf16[1,32,2,128]{3,2,1,0:T(2,128)(2,1)S(1)}, u32[]{:S(2)}, u32[]{:S(2)}) collective-permute-start(bf16[1,32,2,128]{3,2,1,0:T(2,128)(2,1)S(1)} %get-tuple-element.275), channel_id=1, source_target_pairs={{16,0},{32,16},{48,32},{64,48},{80,64},{96,80},{112,96},{128,112},... | collective-permute-start | bytes 49160 | tf_op jit(solution)/shard_map/ppermute | solution.py:17
  33.2 3.4 %collective-permute-start.6 = (bf16[34,1,2,128]{3,2,1,0:T(2,128)(2,1)S(1)}, bf16[34,1,2,128]{3,2,1,0:T(2,128)(2,1)S(1)}, u32[]{:S(2)}, u32[]{:S(2)}) collective-permute-start(bf16[34,1,2,128]{3,2,1,0:T(2,128)(2,1)S(1)} %get-tuple-element.271), channel_id=1, source_target_pairs={{0,1},{1,2},{2,3},{3,4},{4,5},{5,6},{6,7},{7,8},{8,9},{9,10},{10,1... | collective-permute-start | bytes 52232 | tf_op jit(solution)/shard_map/ppermute | solution.py:15
  36.5 4.0 %collective-permute-start.7 = (bf16[34,1,2,128]{3,2,1,0:T(2,128)(2,1)S(1)}, bf16[34,1,2,128]{3,2,1,0:T(2,128)(2,1)S(1)}, u32[]{:S(2)}, u32[]{:S(2)}) collective-permute-start(bf16[34,1,2,128]{3,2,1,0:T(2,128)(2,1)S(1)} %get-tuple-element.270), channel_id=1, source_target_pairs={{1,0},{2,1},{3,2},{4,3},{5,4},{6,5},{7,6},{8,7},{9,8},{10,9},{11,1... | collective-permute-start | bytes 52232 | tf_op jit(solution)/shard_map/ppermute | solution.py:17
  42.9 4.3 %collective-permute-start.2 = (bf16[36,2,256]{2,1,0:T(2,128)(2,1)S(1)}, bf16[36,2,256]{2,1,0:T(2,128)(2,1)S(1)}, u32[]{:S(2)}, u32[]{:S(2)}) collective-permute-start(bf16[36,2,256]{2,1,0:T(2,128)(2,1)S(1)} %get-tuple-element.256), channel_id=1, source_target_pairs={{0,1},{1,2},{2,3},{3,4},{4,5},{5,6},{6,7},{7,8},{8,9},{9,10},{10,1... | collective-permute-start | bytes 110600 | tf_op jit(solution)/shard_map/ppermute | solution.py:15
  47.2 3.1 %collective-permute-start.3 = (bf16[36,2,256]{2,1,0:T(2,128)(2,1)S(1)}, bf16[36,2,256]{2,1,0:T(2,128)(2,1)S(1)}, u32[]{:S(2)}, u32[]{:S(2)}) collective-permute-start(bf16[36,2,256]{2,1,0:T(2,128)(2,1)S(1)} %get-tuple-element.257), channel_id=1, source_target_pairs={{1,0},{2,1},{3,2},{4,3},{5,4},{6,5},{7,6},{8,7},{9,8},{10,9},{11,1... | collective-permute-start | bytes 110600 | tf_op jit(solution)/shard_map/ppermute | solution.py:17
  52.6 61.0 %collective-permute-done.6 = bf16[34,1,2,128]{3,2,1,0:T(2,128)(2,1)S(1)} collective-permute-done((bf16[34,1,2,128]{3,2,1,0:T(2,128)(2,1)S(1)}, bf16[34,1,2,128]{3,2,1,0:T(2,128)(2,1)S(1)}, u32[]{:S(2)}, u32[]{:S(2)}) %collective-permute-start.6) | collective-permute-done | bytes 17440 | tf_op jit(solution)/shard_map/ppermute | solution.py:15
  113.6 3.5 %collective-permute-done.7 = bf16[34,1,2,128]{3,2,1,0:T(2,128)(2,1)S(1)} collective-permute-done((bf16[34,1,2,128]{3,2,1,0:T(2,128)(2,1)S(1)}, bf16[34,1,2,128]{3,2,1,0:T(2,128)(2,1)S(1)}, u32[]{:S(2)}, u32[]{:S(2)}) %collective-permute-start.7) | collective-permute-done | bytes 17440 | tf_op jit(solution)/shard_map/ppermute | solution.py:17
  119.2 4.3 %fusion.115 = (bf16[32,32,2,128]{3,2,1,0:T(2,128)(2,1)}, bf16[32,32,2,128]{3,2,1,0:T(2,128)(2,1)}, bf16[32,32,2,128]{3,2,1,0:T(2,128)(2,1)}, bf16[32,32,2,128]{3...) fusion(bf16[34,33,2,128]{3,2,1,0:T(2,128)(2,1)S(1)} %get-tuple-element.268, ...), kind=kLoop, calls=%fused_computation.264 | loop fusion | bytes 6291456 | tf_op jit(solution)/shard_map/slice | solution.py:133
  129.8 2.5 fusion.32
  132.2 2.4 fusion.30
  134.7 4.9 %copy.31 = bf16[16,16,16,512]{3,2,0,1:T(8,128)(2,1)} copy(bf16[16,16,16,512]{3,2,1,0:T(8,128)(2,1)} %all-to-all-done) | data formatting | bytes 8388608 | tf_op jit(solution)/shard_map/all_to_all | solution.py:110
  139.6 92.8 %while.14 = (s32[]{:T(128)}, f32[256,512]{1,0:T(8,128)S(1)}, s32[16,16]{1,0:T(8,128)S(1)}, s32[16,16,16]{1,0,2:T(8,128)}, f32[64,512]{1,0:T(8,128)S(1)}, /*index...) while((s32[]{:T(128)}, f32[256,512]{1,0:T(8,128)S(1)}, ...), condition=%wide.region_1.2_spmd.clone, body=%wide.region_0.1_spmd.clone.sunk | while | flops 101862912 | bytes 4610671 | solution.py:59
  140.5 3.9 %gather_fusion = bf16[256,512]{1,0:T(8,128)(2,1)S(1)} fusion(bf16[4096,512]{1,0:T(8,128)(2,1)} %get-tuple-element.398, s32[1024]{0:T(1024)S(1)} %pad_clamp_fusion.2), kind=kCustom, calls=%fused_computation.clone.clone.1 | custom fusion | bytes 525312 | tf_op jit(solution)/shard_map/while/body/eval_jaxpr/jit(_take)/gather | solution.py:47
  146.3 3.9 %gather_fusion = bf16[256,512]{1,0:T(8,128)(2,1)S(1)} fusion(bf16[4096,512]{1,0:T(8,128)(2,1)} %get-tuple-element.398, s32[1024]{0:T(1024)S(1)} %pad_clamp_fusion.2), kind=kCustom, calls=%fused_computation.clone.clone.1 | custom fusion | bytes 525312 | tf_op jit(solution)/shard_map/while/body/eval_jaxpr/jit(_take)/gather | solution.py:47
  152.1 3.9 %gather_fusion = bf16[256,512]{1,0:T(8,128)(2,1)S(1)} fusion(bf16[4096,512]{1,0:T(8,128)(2,1)} %get-tuple-element.398, s32[1024]{0:T(1024)S(1)} %pad_clamp_fusion.2), kind=kCustom, calls=%fused_computation.clone.clone.1 | custom fusion | bytes 525312 | tf_op jit(solution)/shard_map/while/body/eval_jaxpr/jit(_take)/gather | solution.py:47
  157.9 3.9 %gather_fusion = bf16[256,512]{1,0:T(8,128)(2,1)S(1)} fusion(bf16[4096,512]{1,0:T(8,128)(2,1)} %get-tuple-element.398, s32[1024]{0:T(1024)S(1)} %pad_clamp_fusion.2), kind=kCustom, calls=%fused_computation.clone.clone.1 | custom fusion | bytes 525312 | tf_op jit(solution)/shard_map/while/body/eval_jaxpr/jit(_take)/gather | solution.py:47
  163.6 3.9 %gather_fusion = bf16[256,512]{1,0:T(8,128)(2,1)S(1)} fusion(bf16[4096,512]{1,0:T(8,128)(2,1)} %get-tuple-element.398, s32[1024]{0:T(1024)S(1)} %pad_clamp_fusion.2), kind=kCustom, calls=%fused_computation.clone.clone.1 | custom fusion | bytes 525312 | tf_op jit(solution)/shard_map/while/body/eval_jaxpr/jit(_take)/gather | solution.py:47
  169.4 3.9 %gather_fusion = bf16[256,512]{1,0:T(8,128)(2,1)S(1)} fusion(bf16[4096,512]{1,0:T(8,128)(2,1)} %get-tuple-element.398, s32[1024]{0:T(1024)S(1)} %pad_clamp_fusion.2), kind=kCustom, calls=%fused_computation.clone.clone.1 | custom fusion | bytes 525312 | tf_op jit(solution)/shard_map/while/body/eval_jaxpr/jit(_take)/gather | solution.py:47
  175.2 3.9 %gather_fusion = bf16[256,512]{1,0:T(8,128)(2,1)S(1)} fusion(bf16[4096,512]{1,0:T(8,128)(2,1)} %get-tuple-element.398, s32[1024]{0:T(1024)S(1)} %pad_clamp_fusion.2), kind=kCustom, calls=%fused_computation.clone.clone.1 | custom fusion | bytes 525312 | tf_op jit(solution)/shard_map/while/body/eval_jaxpr/jit(_take)/gather | solution.py:47
  181.0 3.9 %gather_fusion = bf16[256,512]{1,0:T(8,128)(2,1)S(1)} fusion(bf16[4096,512]{1,0:T(8,128)(2,1)} %get-tuple-element.398, s32[1024]{0:T(1024)S(1)} %pad_clamp_fusion.2), kind=kCustom, calls=%fused_computation.clone.clone.1 | custom fusion | bytes 525312 | tf_op jit(solution)/shard_map/while/body/eval_jaxpr/jit(_take)/gather | solution.py:47
  186.8 3.9 %gather_fusion = bf16[256,512]{1,0:T(8,128)(2,1)S(1)} fusion(bf16[4096,512]{1,0:T(8,128)(2,1)} %get-tuple-element.398, s32[1024]{0:T(1024)S(1)} %pad_clamp_fusion.2), kind=kCustom, calls=%fused_computation.clone.clone.1 | custom fusion | bytes 525312 | tf_op jit(solution)/shard_map/while/body/eval_jaxpr/jit(_take)/gather | solution.py:47
  192.6 3.9 %gather_fusion = bf16[256,512]{1,0:T(8,128)(2,1)S(1)} fusion(bf16[4096,512]{1,0:T(8,128)(2,1)} %get-tuple-element.398, s32[1024]{0:T(1024)S(1)} %pad_clamp_fusion.2), kind=kCustom, calls=%fused_computation.clone.clone.1 | custom fusion | bytes 525312 | tf_op jit(solution)/shard_map/while/body/eval_jaxpr/jit(_take)/gather | solution.py:47
  198.4 3.9 %gather_fusion = bf16[256,512]{1,0:T(8,128)(2,1)S(1)} fusion(bf16[4096,512]{1,0:T(8,128)(2,1)} %get-tuple-element.398, s32[1024]{0:T(1024)S(1)} %pad_clamp_fusion.2), kind=kCustom, calls=%fused_computation.clone.clone.1 | custom fusion | bytes 525312 | tf_op jit(solution)/shard_map/while/body/eval_jaxpr/jit(_take)/gather | solution.py:47
  204.2 3.9 %gather_fusion = bf16[256,512]{1,0:T(8,128)(2,1)S(1)} fusion(bf16[4096,512]{1,0:T(8,128)(2,1)} %get-tuple-element.398, s32[1024]{0:T(1024)S(1)} %pad_clamp_fusion.2), kind=kCustom, calls=%fused_computation.clone.clone.1 | custom fusion | bytes 525312 | tf_op jit(solution)/shard_map/while/body/eval_jaxpr/jit(_take)/gather | solution.py:47
  210.0 3.9 %gather_fusion = bf16[256,512]{1,0:T(8,128)(2,1)S(1)} fusion(bf16[4096,512]{1,0:T(8,128)(2,1)} %get-tuple-element.398, s32[1024]{0:T(1024)S(1)} %pad_clamp_fusion.2), kind=kCustom, calls=%fused_computation.clone.clone.1 | custom fusion | bytes 525312 | tf_op jit(solution)/shard_map/while/body/eval_jaxpr/jit(_take)/gather | solution.py:47
  215.8 3.9 %gather_fusion = bf16[256,512]{1,0:T(8,128)(2,1)S(1)} fusion(bf16[4096,512]{1,0:T(8,128)(2,1)} %get-tuple-element.398, s32[1024]{0:T(1024)S(1)} %pad_clamp_fusion.2), kind=kCustom, calls=%fused_computation.clone.clone.1 | custom fusion | bytes 525312 | tf_op jit(solution)/shard_map/while/body/eval_jaxpr/jit(_take)/gather | solution.py:47
  221.6 3.9 %gather_fusion = bf16[256,512]{1,0:T(8,128)(2,1)S(1)} fusion(bf16[4096,512]{1,0:T(8,128)(2,1)} %get-tuple-element.398, s32[1024]{0:T(1024)S(1)} %pad_clamp_fusion.2), kind=kCustom, calls=%fused_computation.clone.clone.1 | custom fusion | bytes 525312 | tf_op jit(solution)/shard_map/while/body/eval_jaxpr/jit(_take)/gather | solution.py:47
  227.4 3.9 %gather_fusion = bf16[256,512]{1,0:T(8,128)(2,1)S(1)} fusion(bf16[4096,512]{1,0:T(8,128)(2,1)} %get-tuple-element.398, s32[1024]{0:T(1024)S(1)} %pad_clamp_fusion.2), kind=kCustom, calls=%fused_computation.clone.clone.1 | custom fusion | bytes 525312 | tf_op jit(solution)/shard_map/while/body/eval_jaxpr/jit(_take)/gather | solution.py:47
  235.3 6.5 %fusion.74 = f32[1024,256]{1,0:T(8,128)S(1)} fusion(bf16[256,256]{1,0:T(8,128)(2,1)S(1)} %copy-done.15, f32[1024,256]{1,0:T(8,128)S(1)} %reshape.260, f32[1024,128]{1,0:T(8,128)} %bitcast.278, f32[1024,128]{1,0:T(8,128)} %bitcast.279, f32[1024,128]{1,0:T(8,128)} %bitcast.280, f32[1024,128]{1,0:T(8,128)} %bitcast.281, f32[1024,128]{1,0:T(8,128)} %bitcast.291, ...), kind=kOutput, calls=%fused_computation.182 | convolution fusion | flops 142868480 | bytes 19005440 | tf_op jit(solution)/shard_map/dot_general | solution.py:126
  (308 shorter events, 68.1 us)
Async XLA Ops:
  0.0 3.7 %copy-start = (bf16[256,256]{1,0:T(8,128)(2,1)S(1)}, bf16[256,256]{1,0:T(8,128)(2,1)}, u32[]{:S(2)}) copy-start(bf16[256,256]{1,0:T(8,128)(2,1)} %param.16) | copy-start | bytes 393220
  5.3 1.2 copy-start.13
  10.0 21.4 %copy-start.19 = (f32[16,2,128]{2,1,0:T(2,128)S(1)}, f32[16,2,128]{2,1,0:T(2,128)}, u32[]{:S(2)}) copy-start(f32[16,2,128]{2,1,0:T(2,128)} %param.18) | copy-start | bytes 49156
  10.0 21.5 %copy-start.16 = (f32[64,2,256]{2,1,0:T(2,128)S(1)}, f32[64,2,256]{2,1,0:T(2,128)}, u32[]{:S(2)}) copy-start(f32[64,2,256]{2,1,0:T(2,128)} %param.23) | copy-start | bytes 393220
  10.0 21.5 %copy-start.17 = (s32[16,16,16]{2,1,0:T(8,128)S(1)}, s32[16,16,16]{2,1,0:T(8,128)}, u32[]{:S(2)}) copy-start(s32[16,16,16]{2,1,0:T(8,128)} %param.21) | copy-start | bytes 49156
  10.0 22.3 %copy-start.18 = (s32[16,16,16]{2,1,0:T(8,128)S(1)}, s32[16,16,16]{2,1,0:T(8,128)}, u32[]{:S(2)}) copy-start(s32[16,16,16]{2,1,0:T(8,128)} %param.20) | copy-start | bytes 49156
  10.0 124.6 %all-to-all-start = ((bf16[16,16,16,512]{3,2,1,0:T(8,128)(2,1)}), bf16[16,16,16,512]{3,2,1,0:T(8,128)(2,1)}, u32[]{:S(2)}, u32[]{:S(2)}) async-start(bf16[16,16,16,512]{3,2,1,0:T(8,128)(2,1)} %stack.18), calls=%async_computation | async-start | bytes 8388608 | tf_op jit(solution)/shard_map/all_to_all | solution.py:110
  20.3 22.6 %collective-permute-start = (bf16[2,32,256]{2,1,0:T(8,128)(2,1)S(1)}, bf16[2,32,256]{2,1,0:T(8,128)(2,1)S(1)}, u32[]{:S(2)}, u32[]{:S(2)}) collective-permute-start(bf16[2,32,256]{2,1,0:T(8,128)(2,1)S(1)} %bitcast.306), channel_id=1, source_target_pairs={{0,16},{16,32},{32,48},{48,64},{64,80},{80,96},{96,112},{112,128},... | collective-permute-start | bytes 98312 | tf_op jit(solution)/shard_map/ppermute | solution.py:15
  22.2 20.7 %collective-permute-start.1 = (bf16[2,32,256]{2,1,0:T(8,128)(2,1)S(1)}, bf16[2,32,256]{2,1,0:T(8,128)(2,1)S(1)}, u32[]{:S(2)}, u32[]{:S(2)}) collective-permute-start(bf16[2,32,256]{2,1,0:T(8,128)(2,1)S(1)} %bitcast.305), channel_id=1, source_target_pairs={{16,0},{32,16},{48,32},{64,48},{80,64},{96,80},{112,96},{128,112},... | collective-permute-start | bytes 98312 | tf_op jit(solution)/shard_map/ppermute | solution.py:17
  25.9 7.2 %collective-permute-start.4 = (bf16[1,32,2,128]{3,2,1,0:T(2,128)(2,1)S(1)}, bf16[1,32,2,128]{3,2,1,0:T(2,128)(2,1)S(1)}, u32[]{:S(2)}, u32[]{:S(2)}) collective-permute-start(bf16[1,32,2,128]{3,2,1,0:T(2,128)(2,1)S(1)} %get-tuple-element.274), channel_id=1, source_target_pairs={{0,16},{16,32},{32,48},{48,64},{64,80},{80,96},{96,112},{112,128},... | collective-permute-start | bytes 49160 | tf_op jit(solution)/shard_map/ppermute | solution.py:15
  27.8 5.3 %collective-permute-start.5 = (bf16[1,32,2,128]{3,2,1,0:T(2,128)(2,1)S(1)}, bf16[1,32,2,128]{3,2,1,0:T(2,128)(2,1)S(1)}, u32[]{:S(2)}, u32[]{:S(2)}) collective-permute-start(bf16[1,32,2,128]{3,2,1,0:T(2,128)(2,1)S(1)} %get-tuple-element.275), channel_id=1, source_target_pairs={{16,0},{32,16},{48,32},{64,48},{80,64},{96,80},{112,96},{128,112},... | collective-permute-start | bytes 49160 | tf_op jit(solution)/shard_map/ppermute | solution.py:17
  33.2 80.4 %collective-permute-start.6 = (bf16[34,1,2,128]{3,2,1,0:T(2,128)(2,1)S(1)}, bf16[34,1,2,128]{3,2,1,0:T(2,128)(2,1)S(1)}, u32[]{:S(2)}, u32[]{:S(2)}) collective-permute-start(bf16[34,1,2,128]{3,2,1,0:T(2,128)(2,1)S(1)} %get-tuple-element.271), channel_id=1, source_target_pairs={{0,1},{1,2},{2,3},{3,4},{4,5},{5,6},{6,7},{7,8},{8,9},{9,10},{10,1... | collective-permute-start | bytes 52232 | tf_op jit(solution)/shard_map/ppermute | solution.py:15
  36.5 80.5 %collective-permute-start.7 = (bf16[34,1,2,128]{3,2,1,0:T(2,128)(2,1)S(1)}, bf16[34,1,2,128]{3,2,1,0:T(2,128)(2,1)S(1)}, u32[]{:S(2)}, u32[]{:S(2)}) collective-permute-start(bf16[34,1,2,128]{3,2,1,0:T(2,128)(2,1)S(1)} %get-tuple-element.270), channel_id=1, source_target_pairs={{1,0},{2,1},{3,2},{4,3},{5,4},{6,5},{7,6},{8,7},{9,8},{10,9},{11,1... | collective-permute-start | bytes 52232 | tf_op jit(solution)/shard_map/ppermute | solution.py:17
  42.9 80.6 %collective-permute-start.2 = (bf16[36,2,256]{2,1,0:T(2,128)(2,1)S(1)}, bf16[36,2,256]{2,1,0:T(2,128)(2,1)S(1)}, u32[]{:S(2)}, u32[]{:S(2)}) collective-permute-start(bf16[36,2,256]{2,1,0:T(2,128)(2,1)S(1)} %get-tuple-element.256), channel_id=1, source_target_pairs={{0,1},{1,2},{2,3},{3,4},{4,5},{5,6},{6,7},{7,8},{8,9},{9,10},{10,1... | collective-permute-start | bytes 110600 | tf_op jit(solution)/shard_map/ppermute | solution.py:15
  47.2 76.3 %collective-permute-start.3 = (bf16[36,2,256]{2,1,0:T(2,128)(2,1)S(1)}, bf16[36,2,256]{2,1,0:T(2,128)(2,1)S(1)}, u32[]{:S(2)}, u32[]{:S(2)}) collective-permute-start(bf16[36,2,256]{2,1,0:T(2,128)(2,1)S(1)} %get-tuple-element.257), channel_id=1, source_target_pairs={{1,0},{2,1},{3,2},{4,3},{5,4},{6,5},{7,6},{8,7},{9,8},{10,9},{11,1... | collective-permute-start | bytes 110600 | tf_op jit(solution)/shard_map/ppermute | solution.py:17
  134.7 4.9 %copy-start.14 = (s32[16,16]{1,0:T(8,128)S(1)}, s32[16,16]{1,0:T(8,128)}, u32[]{:S(2)}) copy-start(s32[16,16]{1,0:T(8,128)} %param.22) | copy-start | bytes 3076
  139.6 92.9 %copy-start.12 = (bf16[4,512,256]{2,1,0:T(8,128)(2,1)S(1)}, bf16[4,512,256]{2,1,0:T(8,128)(2,1)}, u32[]{:S(2)}) copy-start(bf16[4,512,256]{2,1,0:T(8,128)(2,1)} %param.24) | copy-start | bytes 3145732
  234.4 0.9 copy-start.15
  235.3 6.5 %copy-start.10 = (bf16[32,32,2,128]{3,2,1,0:T(2,128)(2,1)S(1)}, bf16[32,32,2,128]{3,2,1,0:T(2,128)(2,1)}, u32[]{:S(2)}) copy-start(bf16[32,32,2,128]{3,2,1,0:T(2,128)(2,1)} %get-tuple-element.316) | copy-start | bytes 1572868
  235.3 6.5 %copy-start.11 = (bf16[9,256,256]{2,1,0:T(8,128)(2,1)S(1)}, bf16[9,256,256]{2,1,0:T(8,128)(2,1)}, u32[]{:S(2)}) copy-start(bf16[9,256,256]{2,1,0:T(8,128)(2,1)} %param.17) | copy-start | bytes 3538948
  241.9 1.0 copy-start.4
  242.9 1.0 copy-start.9
  243.9 1.0 copy-start.8
  245.3 1.0 copy-start.7
  246.3 1.0 copy-start.6
  247.4 1.0 copy-start.3
  248.4 1.0 copy-start.5
  249.7 1.0 copy-start.2
  250.3 2.0 copy-start.1
